TPU v7x, 32 devices: a whole 2x2x4 slice. The times are simulated.
32 devices in a mesh: dev: 32 (over z, y, x, core).
Axes of the slice: x: 2, y: 2, z: 4, core: 2. Of those that a mesh axis runs over, the one named last changes fastest.
Arguments:
- layer_input: bfloat16 [5120, 1024], P('dev'), may hold values from -6 to 6
- ln1_gain: bfloat16 [1024], P('dev'), may hold values from 0.5 to 1.5
- ln1_bias: bfloat16 [1024], P('dev'), may hold values from -3 to 3
- qkv_weight: bfloat16 [1024, 3072], P('dev'), may hold values from -1.40625 to 1.40625
- qkv_bias: bfloat16 [3072], P('dev'), may hold values from -3 to 3
- dense_weight: bfloat16 [1024, 1024], P('dev'), may hold values from -0.75 to 0.75
- dense_bias: bfloat16 [1024], P('dev'), may hold values from -3 to 3
- ln2_gain: bfloat16 [1024], P('dev'), may hold values from 0.5 to 1.5
- ln2_bias: bfloat16 [1024], P('dev'), may hold values from -3 to 3
- fc_in_weight: bfloat16 [1024, 4096], P('dev'), may hold values from -0.1875 to 0.1875
- fc_in_bias: bfloat16 [4096], P('dev'), may hold values from -3 to 3
- fc_out_weight: bfloat16 [4096, 1024], P('dev'), may hold values from -0.09375 to 0.09375
- fc_out_bias: bfloat16 [1024], P('dev'), may hold values from -3 to 3
- positions: int32 [5120], P('dev'), may hold values from 0 to 511, as said below
- cotangent: bfloat16 [5120, 1024], P('dev'), may hold values from -6 to 6
Outputs:
- output: bfloat16 [5120, 1024], P('dev')
- grad_input: float32 [5120, 1024], P('dev')
- grad_ln1_gain: float32 [1024], P('dev')
- grad_ln1_bias: float32 [1024], P('dev')
- grad_qkv_weight: float32 [1024, 3072], P('dev')
- grad_qkv_bias: float32 [3072], P('dev')
- grad_dense_weight: float32 [1024, 1024], P('dev')
- grad_dense_bias: float32 [1024], P('dev')
- grad_ln2_gain: float32 [1024], P('dev')
- grad_ln2_bias: float32 [1024], P('dev')
- grad_fc_in_weight: float32 [1024, 4096], P('dev')
- grad_fc_in_bias: float32 [4096], P('dev')
- grad_fc_out_weight: float32 [4096, 1024], P('dev')
- grad_fc_out_bias: float32 [1024], P('dev')
Inputs may be any that keep to these rules, and one draw needn't show every extreme that they name: `positions`: documents lie end to end over all tokens; a token of position p has the p tokens before it in its document, and a token of position 0 starts a document; no document is longer than 512 tokens, and in every draw one document has exactly 512 tokens.
All inputs are finite; a program needn't handle non-finite values.
Results may differ from a plain program's by a relative error of at most 0.0095.
Values may be sent and summed in bfloat16 or wider, within the bound.
A program may use at most 256 MiB of HBM per device.

v0:
```python
import jax
import jax.numpy as jnp
from jax import lax
from jax.sharding import PartitionSpec as P

HEADS = 16
HD = 64
ROT = 16
BACK = 4


EPSILON = 1e-05
ROPE_BASE = 10000.0


def passed_along(block, axis, distance):
    devices = range(lax.axis_size(axis))
    route = [(i - distance, i) for i in devices if i - distance in devices]
    return lax.ppermute(block, axis, route)


def norm_stats(inputs):
    values_f = inputs.astype(jnp.float32)
    centre = jnp.mean(values_f, axis=-1, keepdims=True)
    shifted = values_f - centre
    variance = jnp.mean(shifted * shifted, axis=-1, keepdims=True)
    inv_scale = lax.rsqrt(variance + EPSILON)
    return (shifted * inv_scale, inv_scale)


def rotary_tables(positions, rot_half):
    counter = jnp.arange(rot_half).astype(jnp.float32)
    frequency = ROPE_BASE ** (-2.0 * counter / (2.0 * rot_half))
    angles = positions.astype(jnp.float32)[:, None] * frequency[None, :]
    return (jnp.cos(angles), jnp.sin(angles))


def rotate(head_rows, cos_table, sin_table, orient):
    halfway = cos_table.shape[-1]
    leading = head_rows[..., :halfway]
    trailing = head_rows[..., halfway : 2 * halfway]
    remainder = head_rows[..., 2 * halfway :]
    cosine = cos_table[:, None, :]
    sine_part = orient * sin_table[:, None, :]
    return jnp.concatenate(
        [
            leading * cosine - trailing * sine_part,
            trailing * cosine + leading * sine_part,
            remainder,
        ],
        axis=-1,
    )


def gelu_pair(pre_act):
    cumulative = 0.5 * (1.0 + lax.erf(pre_act * 0.7071067811865476))
    density = jnp.exp(-0.5 * pre_act * pre_act) * 0.3989422804014327
    return (pre_act * cumulative, cumulative + pre_act * density)


def row_sum_product(left_side, right_side):
    return lax.dot_general(
        left_side, right_side, (((0,), (0,)), ((), ())), preferred_element_type=jnp.float32
    )


def times_transpose(left_side, right_side):
    return lax.dot_general(
        left_side, right_side, (((1,), (1,)), ((), ())), preferred_element_type=jnp.float32
    )


def masked_scores(queries, keys_rot, allowed):
    scores = jnp.einsum(
        "qhd,khd->hqk", queries, keys_rot, preferred_element_type=jnp.float32
    ) * HD ** (-0.5)
    return jnp.where(allowed[None], scores, -jnp.inf)


def attend(queries, keys_rot, values_v, allowed):
    scores = masked_scores(queries, keys_rot, allowed)
    row_max = jnp.max(scores, axis=-1, keepdims=True)
    exp_total = jnp.sum(jnp.exp(scores - row_max), axis=-1, keepdims=True)
    log_total = row_max + jnp.log(exp_total)
    probs_b = jnp.exp(scores - log_total).astype(jnp.bfloat16)
    context = jnp.einsum("hqk,khd->qhd", probs_b, values_v, preferred_element_type=jnp.float32)
    return (context, log_total)


def attend_back(queries, keys_rot, values_v, allowed, log_total, grad_context):
    scores = masked_scores(queries, keys_rot, allowed)
    probs = jnp.exp(scores - log_total)
    probs_b = probs.astype(jnp.bfloat16)
    grad_probs = jnp.einsum(
        "qhd,khd->hqk", grad_context, values_v, preferred_element_type=jnp.float32
    )
    row_dot = jnp.sum(probs * grad_probs, axis=-1, keepdims=True)
    grad_scores = (probs * (grad_probs - row_dot) * HD ** (-0.5)).astype(jnp.bfloat16)
    grad_queries = jnp.einsum(
        "hqk,khd->qhd", grad_scores, keys_rot, preferred_element_type=jnp.float32
    )
    grad_keys = jnp.einsum("hqk,qhd->khd", grad_scores, queries, preferred_element_type=jnp.float32)
    grad_values = jnp.einsum(
        "hqk,qhd->khd", probs_b, grad_context, preferred_element_type=jnp.float32
    )
    return (grad_queries, grad_keys, grad_values)


def body(
    layer_input,
    ln1_gain,
    ln1_bias,
    qkv_weight,
    qkv_bias,
    dense_weight,
    dense_bias,
    ln2_gain,
    ln2_bias,
    fc_in_weight,
    fc_in_bias,
    fc_out_weight,
    fc_out_bias,
    positions,
    cotangent,
):
    tok_rows = layer_input.shape[0]
    model_width = layer_input.shape[1]
    normed, inv_scale = norm_stats(layer_input)
    piece_gain_one = lax.all_gather(ln1_gain, "dev", axis=0, tiled=True)
    piece_shift_one = lax.all_gather(ln1_bias, "dev", axis=0, tiled=True)
    piece_qkv = lax.all_gather(qkv_weight, "dev", axis=0, tiled=True)
    piece_gain_two = lax.all_gather(ln2_gain, "dev", axis=0, tiled=True)
    piece_shift_two = lax.all_gather(ln2_bias, "dev", axis=0, tiled=True)
    piece_in = lax.all_gather(fc_in_weight, "dev", axis=0, tiled=True)
    part_attn = (
        normed * piece_gain_one.astype(jnp.float32) + piece_shift_one.astype(jnp.float32)
    ).astype(jnp.bfloat16)
    part_mlp = (
        normed * piece_gain_two.astype(jnp.float32) + piece_shift_two.astype(jnp.float32)
    ).astype(jnp.bfloat16)
    sum_qkv = jnp.dot(part_attn, piece_qkv, preferred_element_type=jnp.float32)
    sum_in = jnp.dot(part_mlp, piece_in, preferred_element_type=jnp.float32)
    out_parts = (
        lax.all_gather(qkv_bias, "dev", axis=0, tiled=True),
        lax.all_gather(dense_weight, "dev", axis=0, tiled=True),
        lax.all_gather(dense_bias, "dev", axis=0, tiled=True),
        lax.all_gather(fc_in_bias, "dev", axis=0, tiled=True),
        lax.all_gather(fc_out_weight, "dev", axis=0, tiled=True),
        lax.all_gather(fc_out_bias, "dev", axis=0, tiled=True),
    )
    bias_qkv = out_parts[0].astype(jnp.float32)
    full_dense = out_parts[1]
    bias_dense = out_parts[2].astype(jnp.float32)
    bias_in = out_parts[3].astype(jnp.float32)
    full_out = out_parts[4]
    bias_out = out_parts[5].astype(jnp.float32)
    mixed_qkv = sum_qkv + bias_qkv
    pre_act = sum_in + bias_in
    cos_table, sin_table = rotary_tables(positions, ROT // 2)
    queries = rotate(
        mixed_qkv[:, :model_width].reshape(tok_rows, HEADS, HD), cos_table, sin_table, 1.0
    ).astype(jnp.bfloat16)
    keys_own = rotate(
        mixed_qkv[:, model_width : 2 * model_width].reshape(tok_rows, HEADS, HD),
        cos_table,
        sin_table,
        1.0,
    ).astype(jnp.bfloat16)
    values_own = mixed_qkv[:, 2 * model_width :].astype(jnp.bfloat16)
    kv_own = jnp.concatenate([keys_own.reshape(tok_rows, model_width), values_own], axis=1)
    earlier = [passed_along(kv_own, "dev", offset) for offset in range(BACK, 0, -1)]
    window = jnp.concatenate(earlier + [kv_own], axis=0)
    win_rows = window.shape[0]
    win_keys = window[:, :model_width].reshape(win_rows, HEADS, HD)
    win_values = window[:, model_width:].reshape(win_rows, HEADS, HD)
    query_index = jnp.arange(tok_rows, dtype=jnp.int32) + BACK * tok_rows
    key_index = jnp.arange(win_rows, dtype=jnp.int32)
    spread = query_index[:, None] - key_index[None, :]
    allowed = (spread >= 0) & (spread <= positions[:, None])
    context, log_total = attend(queries, win_keys, win_values, allowed)
    context_b = context.reshape(tok_rows, model_width).astype(jnp.bfloat16)
    attn_out = jnp.dot(context_b, full_dense, preferred_element_type=jnp.float32) + bias_dense
    activated, gelu_slope = gelu_pair(pre_act)
    activated_b = activated.astype(jnp.bfloat16)
    mlp_out = jnp.dot(activated_b, full_out, preferred_element_type=jnp.float32) + bias_out
    result = (layer_input.astype(jnp.float32) + attn_out + mlp_out).astype(jnp.bfloat16)
    regathered = (
        lax.all_gather(ln1_gain, "dev", axis=0, tiled=True),
        lax.all_gather(ln1_bias, "dev", axis=0, tiled=True),
        lax.all_gather(qkv_weight, "dev", axis=0, tiled=True),
        lax.all_gather(dense_weight, "dev", axis=0, tiled=True),
        lax.all_gather(ln2_gain, "dev", axis=0, tiled=True),
        lax.all_gather(ln2_bias, "dev", axis=0, tiled=True),
        lax.all_gather(fc_in_weight, "dev", axis=0, tiled=True),
        lax.all_gather(fc_out_weight, "dev", axis=0, tiled=True),
    )
    gain_one = regathered[0].astype(jnp.float32)
    shift_one = regathered[1].astype(jnp.float32)
    back_qkv = regathered[2]
    back_dense = regathered[3]
    gain_two = regathered[4].astype(jnp.float32)
    shift_two = regathered[5].astype(jnp.float32)
    back_in = regathered[6]
    back_out = regathered[7]
    left_attn = (normed * gain_one + shift_one).astype(jnp.bfloat16)
    left_mlp = (normed * gain_two + shift_two).astype(jnp.bfloat16)
    top_f = cotangent.astype(jnp.float32)
    g_dense_w = row_sum_product(context_b, cotangent)
    g_dense_b = jnp.sum(top_f, axis=0)
    g_out_w = row_sum_product(activated_b, cotangent)
    g_out_b = jnp.sum(top_f, axis=0)
    grad_pre = times_transpose(cotangent, back_out) * gelu_slope
    grad_pre_b = grad_pre.astype(jnp.bfloat16)
    g_in_w = row_sum_product(left_mlp, grad_pre_b)
    g_in_b = jnp.sum(grad_pre, axis=0)
    grad_left_mlp = times_transpose(grad_pre_b, back_in)
    g_gain_two = jnp.sum(grad_left_mlp * normed, axis=0)
    g_shift_two = jnp.sum(grad_left_mlp, axis=0)
    grad_context = (
        times_transpose(cotangent, back_dense).astype(jnp.bfloat16).reshape(tok_rows, HEADS, HD)
    )
    g_queries, g_win_keys, g_win_values = attend_back(
        queries, win_keys, win_values, allowed, log_total, grad_context
    )
    grad_window = jnp.concatenate(
        [g_win_keys.reshape(win_rows, model_width), g_win_values.reshape(win_rows, model_width)],
        axis=1,
    )
    grad_kv = grad_window[BACK * tok_rows :]
    for offset in range(1, BACK + 1):
        low_row = (BACK - offset) * tok_rows
        grad_kv = grad_kv + passed_along(
            grad_window[low_row : low_row + tok_rows].astype(jnp.bfloat16), "dev", -offset
        ).astype(jnp.float32)
    g_queries = rotate(g_queries, cos_table, sin_table, -1.0)
    g_keys = rotate(
        grad_kv[:, :model_width].reshape(tok_rows, HEADS, HD), cos_table, sin_table, -1.0
    )
    grad_qkv = jnp.concatenate(
        [
            g_queries.reshape(tok_rows, model_width),
            g_keys.reshape(tok_rows, model_width),
            grad_kv[:, model_width:],
        ],
        axis=1,
    )
    grad_qkv_b = grad_qkv.astype(jnp.bfloat16)
    g_qkv_w = row_sum_product(left_attn, grad_qkv_b)
    g_qkv_b = jnp.sum(grad_qkv, axis=0)
    grad_left_attn = times_transpose(grad_qkv_b, back_qkv)
    g_gain_one = jnp.sum(grad_left_attn * normed, axis=0)
    g_shift_one = jnp.sum(grad_left_attn, axis=0)
    grad_normed = grad_left_attn * gain_one + grad_left_mlp * gain_two
    grad_in = top_f + inv_scale * (
        grad_normed
        - jnp.mean(grad_normed, axis=-1, keepdims=True)
        - normed * jnp.mean(grad_normed * normed, axis=-1, keepdims=True)
    )
    summed = (
        lax.psum_scatter(g_gain_one, "dev", scatter_dimension=0, tiled=True),
        lax.psum_scatter(g_shift_one, "dev", scatter_dimension=0, tiled=True),
        lax.psum_scatter(g_qkv_w, "dev", scatter_dimension=0, tiled=True),
        lax.psum_scatter(g_qkv_b, "dev", scatter_dimension=0, tiled=True),
        lax.psum_scatter(g_dense_w, "dev", scatter_dimension=0, tiled=True),
        lax.psum_scatter(g_dense_b, "dev", scatter_dimension=0, tiled=True),
        lax.psum_scatter(g_gain_two, "dev", scatter_dimension=0, tiled=True),
        lax.psum_scatter(g_shift_two, "dev", scatter_dimension=0, tiled=True),
        lax.psum_scatter(g_in_w, "dev", scatter_dimension=0, tiled=True),
        lax.psum_scatter(g_in_b, "dev", scatter_dimension=0, tiled=True),
        lax.psum_scatter(g_out_w, "dev", scatter_dimension=0, tiled=True),
        lax.psum_scatter(g_out_b, "dev", scatter_dimension=0, tiled=True),
    )
    return (
        result,
        grad_in,
        summed[0],
        summed[1],
        summed[2],
        summed[3],
        summed[4],
        summed[5],
        summed[6],
        summed[7],
        summed[8],
        summed[9],
        summed[10],
        summed[11],
    )


def solution(mesh):
    in_specs = (
        P("dev", None),
        P("dev"),
        P("dev"),
        P("dev", None),
        P("dev"),
        P("dev", None),
        P("dev"),
        P("dev"),
        P("dev"),
        P("dev", None),
        P("dev"),
        P("dev", None),
        P("dev"),
        P("dev"),
        P("dev", None),
    )
    out_specs = (
        P("dev", None),
        P("dev", None),
        P("dev"),
        P("dev"),
        P("dev", None),
        P("dev"),
        P("dev", None),
        P("dev"),
        P("dev"),
        P("dev"),
        P("dev", None),
        P("dev"),
        P("dev", None),
        P("dev"),
    )
    return jax.shard_map(body, mesh=mesh, in_specs=in_specs, out_specs=out_specs, check_vma=False)
```

profile of v0, /device:TPU:0, one launch (start us, length us, event | category | flops | bytes accessed | tf_op | source)
XLA Modules:
  0.0 1026.6 jit_solution(10616436383654093669)
XLA Ops:
  16.6 43.7 %all-reduce.15 = (bf16[1024]{0:T(1024)(128)(2,1)}, bf16[1024]{0:T(1024)(128)(2,1)}, bf16[1024]{0:T(1024)(128)(2,1)}, bf16[3072]{0:T(1024)(128)(2,1)S(1)}, bf16[1...) all-reduce(bf16[1024]{0:T(1024)(128)(2,1)S(1)} %dynamic-update-slic, ...), channel_id=1, replica_groups=mesh['dev'=32] {'dev'}, use_global_device_ids=true, to_apply=%add.6 | all-reduce | flops 9216 | bytes 36864
  63.4 19.5 %all-gather.6.cloned.1.call-done = bf16[1024,3072]{1,0:T(8,128)(2,1)} async-done(((bf16[32,3072]{1,0:T(8,128)(2,1)}), bf16[1024,3072]{1,0:T(8,128)(2,1)}) %all-gather.6.cloned.1.call-update) | async-done | bytes 6291472 | tf_op jit(solution)/shard_map/all_gather | solution.py:131
  82.9 4.2 convolution_add_fusion.1
  97.9 3.4 collective-permute-start
  103.4 4.3 collective-permute-start.2
  110.7 2.6 collective-permute-start.3
  113.3 32.1 %collective-permute-done = bf16[160,2048]{1,0:T(8,128)(2,1)S(1)} collective-permute-done((bf16[160,2048]{1,0:T(8,128)(2,1)S(1)}, bf16[160,2048]{1,0:T(8,128)(2,1)S(1)}, u32[]{:S(2)}, u32[]{:S(2)}) %collective-permute-start) | collective-permute-done | bytes 655392 | tf_op jit(solution)/shard_map/ppermute | solution.py:19
  147.3 3.2 copy.61
  150.5 2.5 copy.57
  152.9 2.9 fusion.2
  159.6 2.7 convolution_convert_fusion
  162.3 2.7 fusion.110
  168.0 8.1 fusion.72
  176.1 3.6 copy.65
  179.8 6.6 fusion.109
  186.4 27.8 %fusion.8 = f32[16,64,800]{2,1,0:T(8,128)} fusion(f32[16,160,800]{2,1,0:T(8,128)} %fusion.109, f32[16,160,800]{2,1,0:T(8,128)} %copy-done, f32[16,160]{1,0:T(8,128)S(1)} %log_add_fusion, pred[160,800]{1,0:T(8,128)(4,1)S(1)} %copy-done.16, bf16[160,16,48]{0,2,1:T(8,128)(2,1)} %slice.158, bf16[160,16,8]{0,2,1:T(8,128)(2,1)} %get-tuple-element.52, ...), kind=kOutput, calls=%fused_computation.15 | convolution fusion | flops 285658400 | bytes 20126720 | tf_op jit(solution)/shard_map/hqk,qhd->khd/dot_general | solution.py:102
  214.2 5.3 copy.64
  228.9 27.6 %fusion.35 = f32[160,16,64]{0,2,1:T(8,128)} fusion(bf16[800,16,64]{0,2,1:T(8,128)(2,1)} %bitcast.44, f32[16,160,800]{2,1,0:T(8,128)} %fusion.109, f32[16,160,800]{2,1,0:T(8,128)} %copy-done, f32[16,160]{1,0:T(8,128)S(1)} %log_add_fusion, pred[160,800]{1,0:T(8,128)(4,1)S(1)} %copy-done.16), kind=kOutput, calls=%fused_computation.36 | convolution fusion | flops 284675360 | bytes 18816000 | tf_op jit(solution)/shard_map/hqk,khd->qhd/dot_general | solution.py:99
  267.8 6.4 fusion.91
  274.9 87.5 %all-gather = bf16[32,1,128]{2,1,0:T(2,128)(2,1)S(1)} all-gather(bf16[1,1,128]{2,1,0:T(2,128)(2,1)S(1)} %bitcast.59), channel_id=1, replica_groups=mesh['dev'=32] {'dev'}, dimensions={0}, use_global_device_ids=true | all-gather | bytes 8448 | tf_op jit(solution)/shard_map/all_gather | solution.py:147
  362.5 5.1 convolution_add_fusion
  367.6 7.1 fusion.99
  375.0 6.7 fusion.108
  382.8 8.2 fusion.64
  393.4 6.9 fusion.66
  400.3 5.4 fusion.100
  406.8 38.2 %all-reduce.14 = (f32[1024]{0:T(1024)S(1)}, f32[1024]{0:T(1024)S(1)}, f32[3072]{0:T(1024)S(1)}, f32[1024]{0:T(1024)S(1)}, f32[1024]{0:T(1024)S(1)}, /*index=5*/f32[1024]{0:T(1024)S(1)}, f32[4096]{0:T(1024)S(1)}) all-reduce(f32[1024]{0:T(1024)S(1)} %get-tuple-element.56, ...), channel_id=2, replica_groups=mesh['dev'=32] {'dev'}, use_global_device_ids=true, to_apply=%region_8.9.clone | all-reduce | flops 12288 | bytes 98304
  448.6 5.1 convolution_add_fusion.3
  455.0 34.2 %reduce-scatter.7.cloned.1.call-done = f32[32,1024]{1,0:T(8,128)} async-done(((f32[1024,1024]{1,0:T(8,128)}), f32[32,1024]{1,0:T(8,128)}) %reduce-scatter.7.cloned.1.call-update) | async-done | bytes 131088 | tf_op jit(solution)/shard_map/reduce_scatter | solution.py:264
  489.1 157.4 %reduce-scatter.5.cloned.1.call-done = f32[32,3072]{1,0:T(8,128)} async-done(((f32[1024,3072]{1,0:T(8,128)}), f32[32,3072]{1,0:T(8,128)}) %reduce-scatter.5.cloned.1.call-update) | async-done | bytes 393232 | tf_op jit(solution)/shard_map/reduce_scatter | solution.py:262
  646.5 184.7 %reduce-scatter.11.cloned.1.call-done = f32[128,1024]{1,0:T(8,128)} async-done(((f32[4096,1024]{1,0:T(8,128)}), f32[128,1024]{1,0:T(8,128)}) %reduce-scatter.11.cloned.1.call-update) | async-done | bytes 524304 | tf_op jit(solution)/shard_map/reduce_scatter | solution.py:270
  831.1 187.6 %reduce-scatter.9.cloned.1.call-done = f32[32,4096]{1,0:T(8,128)} async-done(((f32[1024,4096]{1,0:T(8,128)}), f32[32,4096]{1,0:T(8,128)}) %reduce-scatter.9.cloned.1.call-update) | async-done | bytes 524304 | tf_op jit(solution)/shard_map/reduce_scatter | solution.py:268
  (169 shorter events, 68.1 us)
Async XLA Ops:
  7.2 75.7 %all-gather.6.cloned.1.call-start = ((), (), s32[]{:S(2)}) async-start(), calls=%async_computation.4 | async-start | bytes 6488064 | tf_op jit(solution)/shard_map/all_gather | solution.py:131
  7.9 157.4 %all-gather.8.cloned.1.call-start = ((), (), s32[]{:S(2)}) async-start(), calls=%async_computation.5 | async-start | bytes 2162688 | tf_op jit(solution)/shard_map/all_gather | solution.py:145
  8.7 353.8 %all-gather.10.cloned.1.call-start = ((), (), s32[]{:S(2)}) async-start(), calls=%async_computation.6 | async-start | bytes 8650752 | tf_op jit(solution)/shard_map/all_gather | solution.py:134
  9.4 365.6 %all-gather.12.cloned.1.call-start = ((), (), s32[]{:S(2)}) async-start(), calls=%async_computation.7 | async-start | bytes 8650752 | tf_op jit(solution)/shard_map/all_gather | solution.py:148
  10.0 479.1 %reduce-scatter.7.cloned.1.call-start = ((), (), s32[]{:S(2)}) async-start(), calls=%async_computation.9 | async-start | bytes 4325376 | tf_op jit(solution)/shard_map/reduce_scatter | solution.py:264
  63.4 30.7 %copy-start.19 = (f32[160,8]{0,1:T(8,128)}, f32[160,8]{0,1:T(8,128)S(1)}, u32[]{:S(2)}) copy-start(f32[160,8]{0,1:T(8,128)S(1)} %get-tuple-element.68) | copy-start | bytes 15364
  91.4 5.3 copy-start.15
  95.7 12.0 %copy-start.22 = (s32[160]{0:T(256)S(1)}, s32[160]{0:T(256)}, u32[]{:S(2)}) copy-start(s32[160]{0:T(256)} %param.28) | copy-start | bytes 1924
  97.9 47.5 %collective-permute-start = (bf16[160,2048]{1,0:T(8,128)(2,1)S(1)}, bf16[160,2048]{1,0:T(8,128)(2,1)S(1)}, u32[]{:S(2)}, u32[]{:S(2)}) collective-permute-start(bf16[160,2048]{1,0:T(8,128)(2,1)S(1)} %pad_maximum_fusion.5), channel_id=1, source_target_pairs={{0,4},{1,5},{2,6},{3,7},{4,8},{5,9},{6,10},{7,11},{8,12},{9,13},{1... | collective-permute-start | bytes 1966088 | tf_op jit(solution)/shard_map/ppermute | solution.py:19
  101.3 44.2 %collective-permute-start.1 = (bf16[160,2048]{1,0:T(8,128)(2,1)S(1)}, bf16[160,2048]{1,0:T(8,128)(2,1)S(1)}, u32[]{:S(2)}, u32[]{:S(2)}) collective-permute-start(bf16[160,2048]{1,0:T(8,128)(2,1)S(1)} %pad_maximum_fusion.5), channel_id=1, source_target_pairs={{0,3},{1,4},{2,5},{3,6},{4,7},{5,8},{6,9},{7,10},{8,11},{9,12},{10... | collective-permute-start | bytes 1966088 | tf_op jit(solution)/shard_map/ppermute | solution.py:19
  103.4 42.1 %collective-permute-start.2 = (bf16[160,2048]{1,0:T(8,128)(2,1)S(1)}, bf16[160,2048]{1,0:T(8,128)(2,1)S(1)}, u32[]{:S(2)}, u32[]{:S(2)}) collective-permute-start(bf16[160,2048]{1,0:T(8,128)(2,1)S(1)} %pad_maximum_fusion.5), channel_id=1, source_target_pairs={{0,2},{1,3},{2,4},{3,5},{4,6},{5,7},{6,8},{7,9},{8,10},{9,11},{10,... | collective-permute-start | bytes 1966088 | tf_op jit(solution)/shard_map/ppermute | solution.py:19
  110.7 34.9 %collective-permute-start.3 = (bf16[160,2048]{1,0:T(8,128)(2,1)S(1)}, bf16[160,2048]{1,0:T(8,128)(2,1)S(1)}, u32[]{:S(2)}, u32[]{:S(2)}) collective-permute-start(bf16[160,2048]{1,0:T(8,128)(2,1)S(1)} %pad_maximum_fusion.5), channel_id=1, source_target_pairs={{0,1},{1,2},{2,3},{3,4},{4,5},{5,6},{6,7},{7,8},{8,9},{9,10},{10,1... | collective-permute-start | bytes 1966088 | tf_op jit(solution)/shard_map/ppermute | solution.py:19
  150.4 5.4 copy-start.3
  165.1 481.4 %reduce-scatter.5.cloned.1.call-start = ((), (), s32[]{:S(2)}) async-start(), calls=%async_computation.8 | async-start | bytes 12976128 | tf_op jit(solution)/shard_map/reduce_scatter | solution.py:262
  168.0 8.1 copy-start.14
  223.5 35.0 %collective-permute-start.4 = (bf16[160,2048]{1,0:T(8,128)(2,1)}, bf16[160,2048]{1,0:T(8,128)(2,1)}, u32[]{:S(2)}, u32[]{:S(2)}) collective-permute-start(bf16[160,2048]{1,0:T(8,128)(2,1)} %get-tuple-element.35), channel_id=1, source_target_pairs={{1,0},{2,1},{3,2},{4,3},{5,4},{6,5},{7,6},{8,7},{9,8},{10,9},{11,1... | collective-permute-start | bytes 1966088 | tf_op jit(solution)/shard_map/ppermute | solution.py:19
  224.8 33.7 %collective-permute-start.7 = (bf16[160,2048]{1,0:T(8,128)(2,1)}, bf16[160,2048]{1,0:T(8,128)(2,1)}, u32[]{:S(2)}, u32[]{:S(2)}) collective-permute-start(bf16[160,2048]{1,0:T(8,128)(2,1)} %get-tuple-element.36), channel_id=1, source_target_pairs={{4,0},{5,1},{6,2},{7,3},{8,4},{9,5},{10,6},{11,7},{12,8},{13,9},{1... | collective-permute-start | bytes 1966088 | tf_op jit(solution)/shard_map/ppermute | solution.py:19
  226.1 32.5 %collective-permute-start.6 = (bf16[160,2048]{1,0:T(8,128)(2,1)}, bf16[160,2048]{1,0:T(8,128)(2,1)}, u32[]{:S(2)}, u32[]{:S(2)}) collective-permute-start(bf16[160,2048]{1,0:T(8,128)(2,1)} %get-tuple-element.37), channel_id=1, source_target_pairs={{3,0},{4,1},{5,2},{6,3},{7,4},{8,5},{9,6},{10,7},{11,8},{12,9},{13... | collective-permute-start | bytes 1966088 | tf_op jit(solution)/shard_map/ppermute | solution.py:19
  227.4 32.1 %collective-permute-start.5 = (bf16[160,2048]{1,0:T(8,128)(2,1)}, bf16[160,2048]{1,0:T(8,128)(2,1)}, u32[]{:S(2)}, u32[]{:S(2)}) collective-permute-start(bf16[160,2048]{1,0:T(8,128)(2,1)} %get-tuple-element.38), channel_id=1, source_target_pairs={{2,0},{3,1},{4,2},{5,3},{6,4},{7,5},{8,6},{9,7},{10,8},{11,9},{12,... | collective-permute-start | bytes 1966088 | tf_op jit(solution)/shard_map/ppermute | solution.py:19
  262.0 5.8 copy-start.5
  263.6 4.2 copy-start.1
  267.5 6.7 copy-start.7
  267.8 6.4 copy-start.9
  274.3 556.9 %reduce-scatter.11.cloned.1.call-start = ((), (), s32[]{:S(2)}) async-start(), calls=%async_computation.11 | async-start | bytes 17301504 | tf_op jit(solution)/shard_map/reduce_scatter | solution.py:270
  362.5 5.1 copy-start.13
  374.7 644.0 %reduce-scatter.9.cloned.1.call-start = ((), (), s32[]{:S(2)}) async-start(), calls=%async_computation.10 | async-start | bytes 17301504 | tf_op jit(solution)/shard_map/reduce_scatter | solution.py:268
  393.3 7.0 copy-start.6
  393.3 7.0 copy-start.8
  393.3 7.0 copy-start.10
  445.7 573.0 %copy-start.28 = (f32[32]{0:T(128)}, f32[32]{0:T(128)S(1)}, u32[]{:S(2)}) copy-start(f32[32]{0:T(128)S(1)} %dynamic-slice.3) | copy-start | bytes 388
  448.6 5.1 copy-start.2
  448.6 5.1 copy-start.18
  (13 other events, 21.8 us)
Sparse Core Ops, SparseCore 0:
  10.8 71.9 all-gather.5
  85.7 79.5 all-gather.7
  168.2 75.6 all-gather.9
  246.5 98.4 all-gather.11
  347.7 141.3 reduce-scatter.6
  495.6 150.8 reduce-scatter.4
  649.3 181.7 reduce-scatter.10
  834.0 184.6 reduce-scatter.8
where the time goes:
time: 1040 us; the launch traced here: 1030 us
  waiting for transfers between devices  619 us (60%)
  blocking collectives  169 us (16%)
  matrix products  137 us (13%)
  local copies, waits for them, and re-layouts  46.8 us (4%)
  other arithmetic  20.3 us (2%)
  starting transfers between devices  18.6 us (2%)
  between operations  15.3 us (1%)
    reduce_scatter x1, waiting for transfers between devices, body(): lax.psum_scatter(g_in_w, 'dev', scatter_dimension=0, tiled=True)  188 us
    reduce_scatter x1, waiting for transfers between devices, body(): lax.psum_scatter(g_out_w, 'dev', scatter_dimension=0, tiled=True)  185 us
    reduce_scatter x1, waiting for transfers between devices, body(): lax.psum_scatter(g_qkv_w, 'dev', scatter_dimension=0, tiled=True)  157 us
    all_gather x1, blocking collectives, body(): lax.all_gather(fc_in_bias, 'dev', axis=0, tiled=True)  87.5 us
    unnamed x2, blocking collectives  81.9 us
    reduce_scatter x1, waiting for transfers between devices, body(): lax.psum_scatter(g_dense_w, 'dev', scatter_dimension=0, tiled=True)  34.2 us
    ppermute x8, waiting for transfers between devices, passed_along(): return lax.ppermute(block, axis, route)  33 us
    dot_general x1, matrix products, attend_back(): jnp.einsum('hqk,qhd->khd', grad_scores, queries, preferred_element_type=j...  27.8 us
  transfers between devices with their start and end apart: 16, of which 7 were waited for; matrix products, arithmetic and copies ran while one was open for 19% of the time, Pallas kernels for 0%

commit v1 on v0

v1 whole, which is shorter than its diff:
```python
import jax
import jax.numpy as jnp
from jax import lax
from jax.sharding import Mesh
from jax.sharding import PartitionSpec as P

HEADS = 16
HD = 64
ROT = 16
REACH = 512
GROUP = 8
BLOCK = 256


EPSILON = 1e-05
ROPE_BASE = 10000.0


def norm_stats(inputs):
    values_f = inputs.astype(jnp.float32)
    centre = jnp.mean(values_f, axis=-1, keepdims=True)
    shifted = values_f - centre
    variance = jnp.mean(shifted * shifted, axis=-1, keepdims=True)
    inv_scale = lax.rsqrt(variance + EPSILON)
    return (shifted * inv_scale, inv_scale)


def rotary_tables(positions, lanes):
    place = jnp.arange(lanes, dtype=jnp.int32) % HD
    counter = (place % (ROT // 2)).astype(jnp.float32)
    frequency = ROPE_BASE ** (-2.0 * counter / ROT)
    frequency = jnp.where(place < ROT, frequency, 0.0)
    angles = positions.astype(jnp.float32)[:, None] * frequency[None, :]
    sine = jnp.sin(angles)
    lower = jnp.where(place < ROT // 2, -sine, 0.0)
    upper = jnp.where(place >= ROT // 2, sine, 0.0)
    return (jnp.cos(angles), lower, upper)


def rotate(rows, tables, orient):
    cosine, lower, upper = tables
    ahead = jnp.roll(rows, -(ROT // 2), axis=1)
    behind = jnp.roll(rows, ROT // 2, axis=1)
    return rows * cosine + orient * (ahead * lower + behind * upper)


def windows(rows, blocks, size, span):
    heads = rows.shape[1] // HD
    cut = jnp.stack([rows[i * size : i * size + span] for i in range(blocks)])
    return cut.reshape(blocks, span, heads, HD).transpose(0, 2, 1, 3)


def unwindow(grads, blocks, size, span):
    parts = span // size
    heads = grads.shape[1]
    rows = grads.transpose(0, 2, 1, 3).reshape(blocks, parts, size, heads * HD)
    total = None
    for part in range(parts):
        piece = jnp.pad(rows[:, part], ((part, parts - 1 - part), (0, 0), (0, 0)))
        total = piece if total is None else total + piece
    return total.reshape((blocks + parts - 1) * size, heads * HD)


def gelu_pair(pre_act):
    cumulative = 0.5 * (1.0 + lax.erf(pre_act * 0.7071067811865476))
    density = jnp.exp(-0.5 * pre_act * pre_act) * 0.3989422804014327
    return (pre_act * cumulative, cumulative + pre_act * density)


def row_sum_product(left_side, right_side):
    return lax.dot_general(
        left_side, right_side, (((0,), (0,)), ((), ())), preferred_element_type=jnp.float32
    )


def times_transpose(left_side, right_side):
    return lax.dot_general(
        left_side, right_side, (((1,), (1,)), ((), ())), preferred_element_type=jnp.float32
    )


def body(
    layer_input,
    ln1_gain,
    ln1_bias,
    qkv_weight,
    qkv_bias,
    dense_weight,
    dense_bias,
    ln2_gain,
    ln2_bias,
    fc_in_weight,
    fc_in_bias,
    fc_out_weight,
    fc_out_bias,
    positions,
    cotangent,
):
    bf = jnp.bfloat16
    f32 = jnp.float32
    outer = lax.axis_size("g")
    inner = lax.axis_size("r")
    count = outer * inner
    rank = lax.axis_index("r")
    tok_rows, width = layer_input.shape
    part_rows = qkv_weight.shape[0]
    share = width // inner
    unit = fc_out_weight.shape[0]
    hidden = outer * unit
    rows = inner * tok_rows

    place = jnp.stack([positions // 256, positions % 256], axis=1).astype(bf)
    place = jnp.pad(place, ((0, 0), (0, 126)))
    tokens = jnp.concatenate([layer_input, cotangent, place], axis=1)
    tokens = lax.all_gather(tokens, "r", axis=0, tiled=True)
    group_in = tokens[:, :width]
    group_top = tokens[:, width : 2 * width]
    place = tokens[:, 2 * width : 2 * width + 2].astype(f32)
    group_pos = (place[:, 0] * 256.0 + place[:, 1]).astype(jnp.int32)

    pieces = jnp.concatenate(
        [
            qkv_weight.reshape(part_rows, 3, inner, share)
            .transpose(2, 0, 1, 3)
            .reshape(inner, part_rows, 3 * share),
            fc_in_weight.reshape(part_rows, outer, inner, unit)
            .transpose(2, 0, 1, 3)
            .reshape(inner, part_rows, hidden),
        ],
        axis=2,
    )
    pieces = lax.all_to_all(pieces, "r", 0, 0)
    pieces = lax.all_gather(pieces, "g", axis=0).reshape(width, 3 * share + hidden)
    w_qkv = pieces[:, : 3 * share]
    w_in = pieces[:, 3 * share :]
    w_out = lax.all_gather(fc_out_weight, "g", axis=0, tiled=True)

    vectors = [ln1_gain, ln1_bias, ln2_gain, ln2_bias, dense_bias, fc_out_bias, qkv_bias, fc_in_bias]
    sizes = [v.shape[0] for v in vectors]
    flat = jnp.concatenate(vectors)
    extra = -(-flat.shape[0] // width)
    flat = jnp.pad(flat, (0, extra * width - flat.shape[0])).reshape(extra, width)
    mixed = lax.all_gather(jnp.concatenate([dense_weight, flat], axis=0), ("g", "r"), axis=0)
    w_dense = mixed[:, :part_rows].reshape(width, width)
    w_dense = lax.dynamic_slice_in_dim(w_dense, rank * share, share, axis=0)
    flat = mixed[:, part_rows:].reshape(count, extra * width)
    full = []
    start = 0
    for size in sizes:
        full.append(flat[:, start : start + size].reshape(count * size).astype(f32))
        start += size
    gain_one, shift_one, gain_two, shift_two, bias_dense, bias_out, bias_qkv, bias_in = full
    bias_qkv = lax.dynamic_index_in_dim(bias_qkv.reshape(3, inner, share), rank, 1, False).reshape(-1)
    bias_in = lax.dynamic_index_in_dim(bias_in.reshape(outer, inner, unit), rank, 1, False).reshape(-1)

    normed, _ = norm_stats(group_in)
    left_attn = (normed * gain_one + shift_one).astype(bf)
    left_mlp = (normed * gain_two + shift_two).astype(bf)

    mixed_qkv = jnp.dot(left_attn, w_qkv, preferred_element_type=f32) + bias_qkv
    tables = rotary_tables(group_pos, 2 * share)
    rotated = rotate(mixed_qkv[:, : 2 * share], tables, 1.0).astype(bf)
    queries = rotated[:, :share]
    kv_own = jnp.concatenate([rotated[:, share:], mixed_qkv[:, 2 * share :].astype(bf)], axis=1)
    onward = [(i, i + 1) for i in range(outer - 1)]
    halo = lax.ppermute(kv_own[rows - REACH :], "g", onward)

    pre_act = jnp.dot(left_mlp, w_in, preferred_element_type=f32) + bias_in
    activated, gelu_slope = gelu_pair(pre_act)
    activated_b = activated.astype(bf)
    mlp_out = jnp.dot(activated_b, w_out, preferred_element_type=f32)
    grad_pre = times_transpose(group_top, w_out) * gelu_slope
    grad_pre_b = grad_pre.astype(bf)
    g_out_w = row_sum_product(activated_b, group_top).astype(bf)
    g_in_w = row_sum_product(left_mlp, grad_pre_b).astype(bf)
    g_in_b = jnp.sum(grad_pre, axis=0)
    grad_left_mlp = times_transpose(grad_pre_b, w_in)
    g_out_w = lax.psum_scatter(g_out_w, "g", scatter_dimension=0, tiled=True).astype(f32)
    g_in_w = lax.psum_scatter(g_in_w, "g", scatter_dimension=0, tiled=True)
    g_in_w = lax.all_to_all(g_in_w.reshape(inner, part_rows, hidden), "r", 0, 0)
    g_in_w = (
        g_in_w.reshape(inner, part_rows, outer, unit)
        .transpose(1, 2, 0, 3)
        .reshape(part_rows, count * unit)
        .astype(f32)
    )

    size = BLOCK
    blocks = rows // size
    span = size + REACH
    reach = jnp.concatenate([halo, kv_own], axis=0)
    q_blocks = windows(queries, blocks, size, size)
    k_blocks = windows(reach[:, :share], blocks, size, span)
    v_blocks = windows(reach[:, share:], blocks, size, span)
    spread = jnp.arange(size, dtype=jnp.int32)[:, None] + REACH - jnp.arange(span, dtype=jnp.int32)[None]
    allowed = (spread >= 0)[None] & (spread[None] <= group_pos.reshape(blocks, size, 1))
    scores = jnp.einsum("nhqd,nhkd->nhqk", q_blocks, k_blocks, preferred_element_type=f32) * HD ** (-0.5)
    scores = jnp.where(allowed[:, None], scores, -jnp.inf)
    row_max = jnp.max(scores, axis=-1, keepdims=True)
    exp_total = jnp.sum(jnp.exp(scores - row_max), axis=-1, keepdims=True)
    probs = jnp.exp(scores - (row_max + jnp.log(exp_total)))
    probs_b = probs.astype(bf)
    context = jnp.einsum("nhqk,nhkd->nhqd", probs_b, v_blocks, preferred_element_type=f32)
    context_b = context.astype(bf).transpose(0, 2, 1, 3).reshape(rows, share)
    attn_out = jnp.dot(context_b, w_dense, preferred_element_type=f32)
    out_part = (attn_out + mlp_out).astype(bf)
    out_sum = lax.psum_scatter(out_part, "r", scatter_dimension=0, tiled=True).astype(f32)
    result = (layer_input.astype(f32) + out_sum + (bias_dense + bias_out)).astype(bf)

    g_dense_w = row_sum_product(context_b, group_top).astype(bf)
    g_dense_w = lax.dynamic_update_slice_in_dim(
        jnp.zeros((width, width), bf), g_dense_w, rank * share, axis=0
    )
    g_dense_w = lax.psum_scatter(g_dense_w, ("g", "r"), scatter_dimension=0, tiled=True).astype(f32)
    grad_context = times_transpose(group_top, w_dense).astype(bf)
    c_blocks = windows(grad_context, blocks, size, size)
    grad_probs = jnp.einsum("nhqd,nhkd->nhqk", c_blocks, v_blocks, preferred_element_type=f32)
    row_dot = jnp.sum(probs * grad_probs, axis=-1, keepdims=True)
    grad_scores = (probs * (grad_probs - row_dot) * HD ** (-0.5)).astype(bf)
    g_q = jnp.einsum("nhqk,nhkd->nhqd", grad_scores, k_blocks, preferred_element_type=f32)
    g_k = jnp.einsum("nhqk,nhqd->nhkd", grad_scores, q_blocks, preferred_element_type=f32)
    g_v = jnp.einsum("nhqk,nhqd->nhkd", probs_b, c_blocks, preferred_element_type=f32)
    g_q = g_q.transpose(0, 2, 1, 3).reshape(rows, share)
    g_kv = jnp.concatenate(
        [unwindow(g_k, blocks, size, span), unwindow(g_v, blocks, size, span)], axis=1
    )
    back = [(i + 1, i) for i in range(outer - 1)]
    returned = lax.ppermute(g_kv[:REACH].astype(bf), "g", back).astype(f32)
    g_kv = g_kv[REACH:] + jnp.pad(returned, ((rows - REACH, 0), (0, 0)))
    g_qk = rotate(jnp.concatenate([g_q, g_kv[:, :share]], axis=1), tables, -1.0)
    grad_qkv = jnp.concatenate([g_qk, g_kv[:, share:]], axis=1)
    grad_qkv_b = grad_qkv.astype(bf)
    g_qkv_w = row_sum_product(left_attn, grad_qkv_b)
    g_qkv_b = jnp.sum(grad_qkv, axis=0)
    grad_left_attn = times_transpose(grad_qkv_b, w_qkv)

    grad_normed = (grad_left_attn * gain_one + grad_left_mlp * gain_two).astype(bf)
    grad_normed = lax.psum_scatter(grad_normed, "r", scatter_dimension=0, tiled=True).astype(f32)

    mine = (jnp.arange(inner) == rank).astype(f32)
    top_f = cotangent.astype(f32)
    sums = [
        jnp.sum(grad_left_attn * normed, axis=0),
        jnp.sum(grad_left_attn, axis=0),
        jnp.sum(grad_left_mlp * normed, axis=0),
        jnp.sum(grad_left_mlp, axis=0),
        jnp.sum(top_f, axis=0),
        (g_qkv_b.reshape(3, 1, share) * mine[None, :, None]).reshape(-1),
        (g_in_b.reshape(outer, 1, unit) * mine[None, :, None]).reshape(-1),
    ]
    lengths = [s.shape[0] // count for s in sums]
    columns = sum(lengths) // part_rows
    table = jnp.concatenate([s.reshape(count, -1) for s in sums], axis=1)
    table = table.reshape(count, columns, part_rows).transpose(0, 2, 1).reshape(width, columns)
    table = jnp.pad(table, ((0, 0), (0, 128 - columns)))
    last = jnp.concatenate([g_qkv_w, table], axis=1).astype(bf)
    last = lax.psum_scatter(last, "g", scatter_dimension=0, tiled=True)
    last = lax.all_to_all(last.reshape(inner, part_rows, 3 * share + 128), "r", 0, 0).astype(f32)
    g_qkv_w = (
        last[:, :, : 3 * share]
        .reshape(inner, part_rows, 3, share)
        .transpose(1, 2, 0, 3)
        .reshape(part_rows, 3 * width)
    )
    table = jnp.sum(last[:, :, 3 * share : 3 * share + columns], axis=0)
    table = table.transpose(1, 0).reshape(-1)
    out = []
    start = 0
    for length in lengths:
        out.append(table[start : start + length])
        start += length

    own_normed, inv_scale = norm_stats(layer_input)
    grad_in = top_f + inv_scale * (
        grad_normed
        - jnp.mean(grad_normed, axis=-1, keepdims=True)
        - own_normed * jnp.mean(grad_normed * own_normed, axis=-1, keepdims=True)
    )
    return (
        result,
        grad_in,
        out[0],
        out[1],
        g_qkv_w,
        out[5],
        g_dense_w,
        out[4],
        out[2],
        out[3],
        g_in_w,
        out[6],
        g_out_w,
        out[4],
    )


def solution(mesh):
    inner = GROUP
    split = Mesh(mesh.devices.reshape(-1, inner), ("g", "r"))
    flat = P(("g", "r"))
    tall = P(("g", "r"), None)
    in_specs = (
        tall, flat, flat, tall, flat, tall, flat, flat, flat, tall, flat, tall, flat, flat, tall,
    )
    out_specs = (
        tall, tall, flat, flat, tall, flat, tall, flat, flat, flat, tall, flat, tall, flat,
    )
    return jax.shard_map(body, mesh=split, in_specs=in_specs, out_specs=out_specs, check_vma=False)
```

time: 1040 us -> 623 us (0.60)
  waiting for transfers between devices: 619 us -> 364 us
  blocking collectives: 169 us -> 14.7 us
  matrix products: 137 us -> 108 us
  other arithmetic: 20.3 us -> 41.8 us
  local copies, waits for them, and re-layouts: 46.8 us -> 59.4 us
    reduce_scatter x4 -> x6, waiting for transfers between devices: 564 us -> 243 us  [the longest x1 132 us: body(): lax.psum_scatter(g_dense_w, ('g', 'r'), scatter_dimension=0, tiled=True)]
    all_gather x4, waiting for transfers between devices: 19.5 us -> 117 us  [the longest x1 38.9 us: body(): lax.all_gather(jnp.concatenate([dense_weight, flat], axis=0), ('g', 'r'),...]
    all_gather x1 -> x0, blocking collectives: 87.5 us -> none  [body(): lax.all_gather(fc_in_bias, 'dev', axis=0, tiled=True)]
    unnamed x2 -> x0, blocking collectives: 81.9 us -> none
    ppermute x8 -> x2, waiting for transfers between devices: 33 us -> 0.01 us  [the longest x1 0.01 us: body(): halo = lax.ppermute(kv_own[rows - REACH:], 'g', onward)]
    dot_general x10, matrix products: 91.3 us -> 75.9 us  [the longest x1 25.4 us: body(): jnp.einsum('nhqk,nhqd->nhkd', grad_scores, q_blocks, preferred_element_ty...]
    all_to_all x0 -> x1, blocking collectives: none -> 14.7 us  [body(): pieces = lax.all_to_all(pieces, 'r', 0, 0)]
    ppermute x8 -> x2, starting transfers between devices: 17.8 us -> 4.69 us  [the longest x1 3.41 us: body(): halo = lax.ppermute(kv_own[rows - REACH:], 'g', onward)]
  transfers between devices with their start and end apart: 16 -> 14, of which waited for: 7 -> 10; matrix products, arithmetic and copies ran while one was open for 19% -> 32% of each run, Pallas kernels for 0% -> 0%
where the time goes in v1:
time: 623 us; the launch traced here: 616 us
  waiting for transfers between devices  364 us (58%)
  matrix products  108 us (17%)
  local copies, waits for them, and re-layouts  59.4 us (10%)
  other arithmetic  41.8 us (7%)
  between operations  15.9 us (3%)
  blocking collectives  14.7 us (2%)
  starting transfers between devices  12.7 us (2%)
    reduce_scatter x1, waiting for transfers between devices, body(): lax.psum_scatter(g_dense_w, ('g', 'r'), scatter_dimension=0, tiled=True)  132 us
    reduce_scatter x1, waiting for transfers between devices, body(): lax.psum_scatter(out_part, 'r', scatter_dimension=0, tiled=True).astype(f32)  45.4 us
    reduce_scatter x1, waiting for transfers between devices, body(): lax.psum_scatter(grad_normed, 'r', scatter_dimension=0, tiled=True)  41.2 us
    all_gather x1, waiting for transfers between devices, body(): lax.all_gather(jnp.concatenate([dense_weight, flat], axis=0), ('g', 'r'),...  38.9 us
    all_gather x1, waiting for transfers between devices, body(): lax.all_gather(pieces, 'g', axis=0).reshape(width, 3 * share + hidden)  38.2 us
    all_gather x1, waiting for transfers between devices, body(): tokens = lax.all_gather(tokens, 'r', axis=0, tiled=True)  36.4 us
    dot_general x1, matrix products, body(): jnp.einsum('nhqk,nhqd->nhkd', grad_scores, q_blocks, preferred_element_ty...  25.4 us
    dot_general x1, matrix products, body(): jnp.einsum('nhqk,nhkd->nhqd', grad_scores, k_blocks, preferred_element_ty...  21.3 us
  transfers between devices with their start and end apart: 14, of which 10 were waited for; matrix products, arithmetic and copies ran while one was open for 32% of the time, Pallas kernels for 0%

profile of v1, /device:TPU:0, one launch (start us, length us, event | category | flops | bytes accessed | tf_op | source)
XLA Modules:
  0.0 616.3 jit_solution(7803772135625668055)
XLA Ops:
  7.2 5.5 concatenate.54
  18.8 14.7 %all_to_all.15 = bf16[8,32,896]{2,1,0:T(8,128)(2,1)} all-to-all(bf16[8,32,896]{2,1,0:T(8,128)(2,1)S(1)} %pad_maximum_fusion.3), channel_id=1, replica_groups=mesh['g'=4,'r'=8] {'r'}, dimensions={0} | all-to-all | bytes 917504 | tf_op jit(solution)/shard_map/all_to_all | solution.py:132
  36.6 38.9 %all-gather.14.cloned.1.call-done = bf16[32,33,1024]{2,1,0:T(8,128)(2,1)} async-done(((bf16[1,33,1024]{2,1,0:T(8,128)(2,1)}), bf16[32,33,1024]{2,1,0:T(8,128)(2,1)}) %all-gather.14.cloned.1.call-update) | async-done | bytes 2162704 | tf_op jit(solution)/shard_map/all_gather | solution.py:143
  79.1 3.2 slice.376
  82.3 36.4 %all-gather.8.cloned.1.call-done = bf16[1280,2176]{1,0:T(8,128)(2,1)} async-done(((bf16[160,2176]{1,0:T(8,128)(2,1)}), bf16[1280,2176]{1,0:T(8,128)(2,1)}) %all-gather.8.cloned.1.call-update) | async-done | bytes 5570576 | tf_op jit(solution)/shard_map/all_gather | solution.py:115
  123.4 38.2 %all-gather.12.cloned.1.call-done = bf16[32,32,896]{2,1,0:T(8,128)(2,1)} async-done(((bf16[8,32,896]{2,1,0:T(8,128)(2,1)}), bf16[32,32,896]{2,1,0:T(8,128)(2,1)}) %all-gather.12.cloned.1.call-update) | async-done | bytes 1835024 | tf_op jit(solution)/shard_map/all_gather | solution.py:133
  161.6 3.5 fusion.163
  167.0 5.9 fusion.69
  174.9 3.4 collective-permute-start
  183.4 5.1 multiply_convert_fusion.1
  188.5 4.0 all-gather.10.cloned.1.call-done
  192.5 5.9 fusion.164
  198.4 3.9 fusion.97
  219.4 4.4 fusion.91
  228.8 5.4 fusion.154
  235.4 25.4 %fusion.60 = f32[5,768,2,64]{1,3,2,0:T(8,128)} fusion(f32[5,2,256,768]{3,2,1,0:T(8,128)} %fusion.91, f32[5,2,256,768]{3,2,1,0:T(8,128)} %copy-done, f32[5,2,256]{2,1,0:T(2,128)} %copy-done.29, pred[5,256,768]{2,1,0:T(8,128)(4,1)S(1)} %compare_and_fusion, bf16[5,256,2,64]{1,3,2,0:T(8,128)(2,1)S(1)} %copy-done.19), kind=kOutput, calls=%fused_computation.74 | convolution fusion | flops 273288448 | bytes 19015680 | tf_op jit(solution)/shard_map/nhqk,nhqd->nhkd/dot_general | solution.py:221
  260.8 4.2 reshape.382
  265.1 5.2 fusion.155
  275.4 21.3 %fusion.80 = f32[5,256,2,64]{1,3,2,0:T(8,128)} fusion(f32[5,2,256,768]{3,2,1,0:T(8,128)} %fusion.91, f32[5,2,256,768]{3,2,1,0:T(8,128)} %copy-done, f32[5,2,256]{2,1,0:T(2,128)S(1)} %copy-done.30, pred[5,256,768]{2,1,0:T(8,128)(4,1)S(1)} %compare_and_fusion, bf16[5,768,2,64]{1,3,2,0:T(8,128)(2,1)} %copy-done.10), kind=kOutput, calls=%fused_computation.94 | convolution fusion | flops 273288448 | bytes 18360320 | tf_op jit(solution)/shard_map/nhqk,nhkd->nhqd/dot_general | solution.py:220
  299.4 5.8 fusion.72
  305.6 6.6 %fusion.14 = (bf16[1024]{0:T(1024)(128)(2,1)S(1)}, bf16[1024]{0:T(1024)(128)(2,1)S(1)}, bf16[1024]{0:T(1024)(128)(2,1)S(1)}, bf16[1024]{0:T(1024)(128)(2,1)S(1)}, bf16[1280,1024]{1,0:T(8,128)(2,1)}) fusion(f32[1280,1024]{1,0:T(8,128)} %fusion.97, f32[1280]{0:T(1024)S(1)} %copy-done.35, f32[1280]{0:T(1024)S(1)} %broadcast_multiply_fusion, ...), kind=kOutput, calls=%fused_computation.21 | convolution fusion | flops 1025634304 | bytes 13264896 | tf_op jit(solution)/shard_map/dot_general | solution.py:77
  314.4 3.2 convolution_convert_fusion.2
  318.8 4.7 fusion.63
  323.9 5.4 fusion.89
  337.6 3.3 add_convert_fusion.1
  342.1 3.9 all-to-all-start.2
  346.2 3.2 reduce-scatter.11.cloned.1.call-done
  352.9 3.4 all-to-all-start.1
  356.5 21.1 %reduce-scatter.17.cloned.1.call-done = bf16[128,1024]{1,0:T(8,128)(2,1)} async-done(((bf16[512,1024]{1,0:T(8,128)(2,1)}), bf16[128,1024]{1,0:T(8,128)(2,1)}) %reduce-scatter.17.cloned.1.call-update) | async-done | bytes 262160 | tf_op jit(solution)/shard_map/reduce_scatter | solution.py:178
  384.5 132.3 %reduce-scatter.13.cloned.1.call-done = bf16[32,1024]{1,0:T(8,128)(2,1)} async-done(((bf16[1024,1024]{1,0:T(8,128)(2,1)}), bf16[32,1024]{1,0:T(8,128)(2,1)}) %reduce-scatter.13.cloned.1.call-update) | async-done | bytes 65552 | tf_op jit(solution)/shard_map/reduce_scatter | solution.py:214
  518.3 41.2 %reduce-scatter.9.cloned.1.call-done = bf16[160,1024]{1,0:T(8,128)(2,1)} async-done(((bf16[1280,1024]{1,0:T(8,128)(2,1)}), bf16[160,1024]{1,0:T(8,128)(2,1)}) %reduce-scatter.9.cloned.1.call-update) | async-done | bytes 327696 | tf_op jit(solution)/shard_map/reduce_scatter | solution.py:238
  560.8 45.4 %reduce-scatter.7.cloned.1.call-done = bf16[160,1024]{1,0:T(8,128)(2,1)} async-done(((bf16[1280,1024]{1,0:T(8,128)(2,1)}), bf16[160,1024]{1,0:T(8,128)(2,1)}) %reduce-scatter.7.cloned.1.call-update) | async-done | bytes 327696 | tf_op jit(solution)/shard_map/reduce_scatter | solution.py:207
  (297 shorter events, 86.4 us)
Async XLA Ops:
  7.2 11.3 %copy-start.26 = (bf16[32,3072]{1,0:T(8,128)(2,1)S(1)}, bf16[32,3072]{1,0:T(8,128)(2,1)}, u32[]{:S(2)}) copy-start(bf16[32,3072]{1,0:T(8,128)(2,1)} %param.18) | copy-start | bytes 589828
  7.2 68.4 %all-gather.14.cloned.1.call-start = ((), (), s32[]{:S(2)}) async-start(), calls=%async_computation.18 | async-start | bytes 2703360 | tf_op jit(solution)/shard_map/all_gather | solution.py:143
  14.2 104.4 %all-gather.8.cloned.1.call-start = ((), (), s32[]{:S(2)}) async-start(), calls=%async_computation.9 | async-start | bytes 6266880 | tf_op jit(solution)/shard_map/all_gather | solution.py:115
  17.2 144.4 %all-gather.12.cloned.1.call-start = ((), (), s32[]{:S(2)}) async-start(), calls=%async_computation.17 | async-start | bytes 2293760 | tf_op jit(solution)/shard_map/all_gather | solution.py:133
  18.3 16.9 %copy-start.5 = (bf16[160,1024]{1,0:T(8,128)(2,1)S(1)}, bf16[160,1024]{1,0:T(8,128)(2,1)}, u32[]{:S(2)}) copy-start(bf16[160,1024]{1,0:T(8,128)(2,1)} %param.29) | copy-start | bytes 983044
  33.6 158.9 %all-gather.10.cloned.1.call-start = ((), (), s32[]{:S(2)}) async-start(), calls=%async_computation.10 | async-start | bytes 1310720 | tf_op jit(solution)/shard_map/all_gather | solution.py:136
  34.2 307.9 %reduce-scatter.15.cloned.1.call-start = ((), (), s32[]{:S(2)}) async-start(), calls=%async_computation.15 | async-start | bytes 1310720 | tf_op jit(solution)/shard_map/reduce_scatter | solution.py:179
  34.2 132.7 %copy-start.46 = (pred[256]{0:T(512)(128)(4,1)}, pred[256]{0:T(512)(128)(4,1)S(1)}, u32[]{:S(2)}) copy-start(pred[256]{0:T(512)(128)(4,1)S(1)} %get-tuple-element.76) | copy-start | bytes 772
  34.2 132.7 %copy-start.48 = (pred[256]{0:T(512)(128)(4,1)}, pred[256]{0:T(512)(128)(4,1)S(1)}, u32[]{:S(2)}) copy-start(pred[256]{0:T(512)(128)(4,1)S(1)} %get-tuple-element.77) | copy-start | bytes 772
  34.3 132.7 %copy-start.44 = (f32[256]{0:T(256)}, f32[256]{0:T(256)S(1)}, u32[]{:S(2)}) copy-start(f32[256]{0:T(256)S(1)} %compare_select_fusion.2) | copy-start | bytes 3076
  35.4 85.4 %copy-start.50 = (f32[8]{0:T(128)}, f32[8]{0:T(128)S(1)}, u32[]{:S(2)}) copy-start(f32[8]{0:T(128)S(1)} %compare_convert_fusion) | copy-start | bytes 100
  77.1 84.5 %copy-start.36 = (f32[1024]{0:T(1024)}, f32[1024]{0:T(1024)S(1)}, u32[]{:S(2)}) copy-start(f32[1024]{0:T(1024)S(1)} %reshape.397) | copy-start | bytes 12292
  77.1 84.4 %copy-start.38 = (f32[1024]{0:T(1024)}, f32[1024]{0:T(1024)S(1)}, u32[]{:S(2)}) copy-start(f32[1024]{0:T(1024)S(1)} %reshape.398) | copy-start | bytes 12292
  123.4 41.7 %copy-start.32 = (f32[1280]{0:T(1024)}, f32[1280]{0:T(1024)S(1)}, u32[]{:S(2)}) copy-start(f32[1280]{0:T(1024)S(1)} %add_rsqrt_fusion) | copy-start | bytes 15364
  165.1 8.9 %copy-start.13 = (bf16[1280,384]{0,1:T(8,128)(2,1)}, bf16[1280,384]{0,1:T(8,128)(2,1)S(1)}, u32[]{:S(2)}) copy-start(bf16[1280,384]{0,1:T(8,128)(2,1)S(1)} %get-tuple-element.68) | copy-start | bytes 2949124
  173.6 8.3 %copy-start.6 = (bf16[1280,128]{0,1:T(8,128)(2,1)}, bf16[1280,128]{0,1:T(8,128)(2,1)S(1)}, u32[]{:S(2)}) copy-start(bf16[1280,128]{0,1:T(8,128)(2,1)S(1)} %slice.368) | copy-start | bytes 983044
  174.1 7.8 %copy-start.8 = (bf16[1280,128]{0,1:T(8,128)(2,1)}, bf16[1280,128]{0,1:T(8,128)(2,1)S(1)}, u32[]{:S(2)}) copy-start(bf16[1280,128]{0,1:T(8,128)(2,1)S(1)} %slice.369) | copy-start | bytes 983044
  174.9 38.0 %collective-permute-start = (bf16[512,256]{0,1:T(8,128)(2,1)}, bf16[512,256]{0,1:T(8,128)(2,1)}, u32[]{:S(2)}, u32[]{:S(2)}) collective-permute-start(bf16[512,256]{0,1:T(8,128)(2,1)} %pad_maximum_fusion.4), channel_id=1, source_target_pairs={{0,8},{8,16},{16,24},{1,9},{9,17},{17,25},{2,10},{10,18},{18,26},{... | collective-permute-start | bytes 786440 | tf_op jit(solution)/shard_map/ppermute | solution.py:166
  183.4 18.9 %slice-start = ((s8[5570560]{0:T(1024)(128)(4,1)}), s8[1376256]{0:T(1024)(128)(4,1)S(1)}, s32[]{:S(2)}) async-start(s8[5570560]{0:T(1024)(128)(4,1)} %bitcast.149), calls=%async_computation.19 | async-start | bytes 2752512
  192.5 9.8 %slice-start.1 = ((s8[5570560]{0:T(1024)(128)(4,1)}), s8[4194304]{0:T(1024)(128)(4,1)S(1)}, s32[]{:S(2)}) async-start(s8[5570560]{0:T(1024)(128)(4,1)} %bitcast.149), calls=%async_computation.20 | async-start | bytes 8388608
  205.2 7.7 %copy-start.7 = (bf16[1280,128]{0,1:T(8,128)(2,1)S(1)}, bf16[1280,128]{0,1:T(8,128)(2,1)}, u32[]{:S(2)}) copy-start(bf16[1280,128]{0,1:T(8,128)(2,1)} %copy-done.6) | copy-start | bytes 983044
  205.2 7.7 %copy-start.9 = (bf16[1280,128]{0,1:T(8,128)(2,1)S(1)}, bf16[1280,128]{0,1:T(8,128)(2,1)}, u32[]{:S(2)}) copy-start(bf16[1280,128]{0,1:T(8,128)(2,1)} %copy-done.8) | copy-start | bytes 983044
  205.2 144.2 %reduce-scatter.11.cloned.1.call-start = ((), (), s32[]{:S(2)}) async-start(), calls=%async_computation.13 | async-start | bytes 1310720 | tf_op jit(solution)/shard_map/reduce_scatter | solution.py:257
  215.9 7.9 %copy-start = (f32[5,2,256,768]{3,2,1,0:T(8,128)}, f32[5,2,256,768]{3,2,1,0:T(8,128)S(1)}, u32[]{:S(2)}) copy-start(f32[5,2,256,768]{3,2,1,0:T(8,128)S(1)} %get-tuple-element.71) | copy-start | bytes 23592964
  274.1 24.3 %collective-permute-start.1 = (bf16[512,256]{0,1:T(8,128)(2,1)}, bf16[512,256]{0,1:T(8,128)(2,1)S(1)}, u32[]{:S(2)}, u32[]{:S(2)}) collective-permute-start(bf16[512,256]{0,1:T(8,128)(2,1)} %fusion.117), channel_id=1, source_target_pairs={{8,0},{16,8},{24,16},{9,1},{17,9},{25,17},{10,2},{18,10},{26,18},{... | collective-permute-start | bytes 786440 | tf_op jit(solution)/shard_map/ppermute | solution.py:228
  318.7 58.8 %reduce-scatter.17.cloned.1.call-start = ((), (), s32[]{:S(2)}) async-start(), calls=%async_computation.16 | async-start | bytes 1310720 | tf_op jit(solution)/shard_map/reduce_scatter | solution.py:178
  323.6 193.2 %reduce-scatter.13.cloned.1.call-start = ((), (), s32[]{:S(2)}) async-start(), calls=%async_computation.14 | async-start | bytes 2162688 | tf_op jit(solution)/shard_map/reduce_scatter | solution.py:214
  333.5 226.1 %reduce-scatter.9.cloned.1.call-start = ((), (), s32[]{:S(2)}) async-start(), calls=%async_computation.12 | async-start | bytes 2949120 | tf_op jit(solution)/shard_map/reduce_scatter | solution.py:238
  334.2 272.0 %reduce-scatter.7.cloned.1.call-start = ((), (), s32[]{:S(2)}) async-start(), calls=%async_computation.11 | async-start | bytes 2949120 | tf_op jit(solution)/shard_map/reduce_scatter | solution.py:207
  342.1 10.8 %all-to-all-start.2 = ((bf16[8,32,512]{2,1,0:T(8,128)(2,1)}), bf16[8,32,512]{2,1,0:T(8,128)(2,1)S(1)}, u32[]{:S(2)}, u32[]{:S(2)}) async-start(bf16[8,32,512]{2,1,0:T(8,128)(2,1)} %bitcast.203), calls=%async_computation.7 | async-start | bytes 524288 | tf_op jit(solution)/shard_map/all_to_all | solution.py:180
  352.9 28.0 %all-to-all-start.1 = ((bf16[8,32,512]{2,1,0:T(8,128)(2,1)}), bf16[8,32,512]{2,1,0:T(8,128)(2,1)S(1)}, u32[]{:S(2)}, u32[]{:S(2)}) async-start(bf16[8,32,512]{2,1,0:T(8,128)(2,1)} %bitcast.46), calls=%async_computation.4 | async-start | bytes 524288 | tf_op jit(solution)/shard_map/all_to_all | solution.py:258
  384.5 224.6 %copy-start.53 = (f32[32]{0:T(128)}, f32[32]{0:T(128)S(1)}, u32[]{:S(2)}) copy-start(f32[32]{0:T(128)S(1)} %get-tuple-element.107) | copy-start | bytes 388
  (41 other events, 152.5 us)
Sparse Core Ops, SparseCore 0:
  14.4 61.1 all-gather.13
  77.4 41.1 all-gather.7
  120.2 41.3 all-gather.11
  163.0 29.4 all-gather.9
  205.3 29.2 reduce-scatter.14
  318.9 30.4 reduce-scatter.10
  351.7 25.7 reduce-scatter.16
  379.8 136.9 reduce-scatter.12
  520.2 39.3 reduce-scatter.8
  562.7 43.4 reduce-scatter.6

commit v2 on v1

--- a/solution.py
+++ b/solution.py
@@ -208,10 +208,16 @@
     result = (layer_input.astype(f32) + out_sum + (bias_dense + bias_out)).astype(bf)
 
     g_dense_w = row_sum_product(context_b, group_top).astype(bf)
+    g_dense_w = lax.psum_scatter(g_dense_w, "g", scatter_dimension=1, tiled=True)
+    stripe = g_dense_w.shape[1]
     g_dense_w = lax.dynamic_update_slice_in_dim(
-        jnp.zeros((width, width), bf), g_dense_w, rank * share, axis=0
-    )
-    g_dense_w = lax.psum_scatter(g_dense_w, ("g", "r"), scatter_dimension=0, tiled=True).astype(f32)
+        jnp.zeros((width, stripe), bf), g_dense_w, rank * share, axis=0
+    )
+    g_dense_w = lax.all_to_all(
+        g_dense_w.reshape(count, part_rows, stripe), ("g", "r"), 0, 0
+    )
+    g_dense_w = g_dense_w.reshape(outer, inner, part_rows, stripe).astype(f32).sum(axis=1)
+    g_dense_w = g_dense_w.transpose(1, 0, 2).reshape(part_rows, width)
     grad_context = times_transpose(group_top, w_dense).astype(bf)
     c_blocks = windows(grad_context, blocks, size, size)
     grad_probs = jnp.einsum("nhqd,nhkd->nhqk", c_blocks, v_blocks, preferred_element_type=f32)

time: 623 us -> 495 us (0.79)
  waiting for transfers between devices: 364 us -> 235 us
  starting transfers between devices: 12.7 us -> 20.4 us
    reduce_scatter x1, waiting for transfers between devices: 132 us -> 0.02 us  [body(): lax.psum_scatter(g_dense_w, 'g', scatter_dimension=1, tiled=True)]
    all_to_all x0 -> x1, waiting for transfers between devices: none -> 18.8 us  [body(): lax.all_to_all(g_dense_w.reshape(count, part_rows, stripe), ('g', 'r'), 0...]
    reduce_scatter x1, waiting for transfers between devices: 21.1 us -> 7.93 us  [body(): lax.psum_scatter(g_out_w, 'g', scatter_dimension=0, tiled=True).astype(f32)]
    all_to_all x0 -> x1, starting transfers between devices: none -> 8.41 us  [body(): lax.all_to_all(g_dense_w.reshape(count, part_rows, stripe), ('g', 'r'), 0...]
  transfers between devices with their start and end apart: 14 -> 15, of which waited for: 10 -> 9; matrix products, arithmetic and copies ran while one was open for 32% -> 37% of each run, Pallas kernels for 0% -> 0%
where the time goes in v2:
time: 495 us; the launch traced here: 488 us
  waiting for transfers between devices  235 us (47%)
  matrix products  106 us (21%)
  local copies, waits for them, and re-layouts  56.8 us (11%)
  other arithmetic  40.2 us (8%)
  starting transfers between devices  20.4 us (4%)
  between operations  15.7 us (3%)
  blocking collectives  14.7 us (3%)
    reduce_scatter x1, waiting for transfers between devices, body(): lax.psum_scatter(out_part, 'r', scatter_dimension=0, tiled=True).astype(f32)  45.4 us
    all_gather x1, waiting for transfers between devices, body(): lax.all_gather(jnp.concatenate([dense_weight, flat], axis=0), ('g', 'r'),...  38.9 us
    reduce_scatter x1, waiting for transfers between devices, body(): lax.psum_scatter(grad_normed, 'r', scatter_dimension=0, tiled=True)  38.5 us
    all_gather x1, waiting for transfers between devices, body(): lax.all_gather(pieces, 'g', axis=0).reshape(width, 3 * share + hidden)  38.2 us
    all_gather x1, waiting for transfers between devices, body(): tokens = lax.all_gather(tokens, 'r', axis=0, tiled=True)  36.3 us
    dot_general x1, matrix products, body(): jnp.einsum('nhqk,nhqd->nhkd', grad_scores, q_blocks, preferred_element_ty...  21.8 us
    dot_general x1, matrix products, body(): jnp.einsum('nhqk,nhkd->nhqd', grad_scores, k_blocks, preferred_element_ty...  21.3 us
    all_to_all x1, waiting for transfers between devices, body(): lax.all_to_all(g_dense_w.reshape(count, part_rows, stripe), ('g', 'r'), 0...  18.8 us
  transfers between devices with their start and end apart: 15, of which 9 were waited for; matrix products, arithmetic and copies ran while one was open for 37% of the time, Pallas kernels for 0%

profile of v2, /device:TPU:0, one launch (start us, length us, event | category | flops | bytes accessed | tf_op | source)
XLA Modules:
  0.0 488.2 jit_solution(6635030356990574684)
XLA Ops:
  7.2 5.5 %concatenate.54 = bf16[416]{0:T(512)(128)(2,1)S(1)} concatenate(bf16[32]{0:T(256)(128)(2,1)} %param.16, bf16[32]{0:T(256)(128)(2,1)} %param.17, bf16[32]{0:T(256)(128)(2,1)} %param.22, bf16[32]{0:T(256)(128)(2,1)} %param.23, bf16[32]{0:T(256)(128)(2,1)} %param.21, bf16[32]{0:T(256)(128)(2,1)} %param.27, bf16[96]{0:T(256)(128)(2,1)} %param.19, bf16[128]{0:T(256)(128)(2,1)} %param.25), dimensions={0} | concatenate | bytes 1664 | tf_op jit(solution)/shard_map/concatenate | solution.py:140
  18.8 14.7 %all_to_all.20 = bf16[8,32,896]{2,1,0:T(8,128)(2,1)} all-to-all(bf16[8,32,896]{2,1,0:T(8,128)(2,1)S(1)} %pad_maximum_fusion.3), channel_id=1, replica_groups=mesh['g'=4,'r'=8] {'r'}, dimensions={0} | all-to-all | bytes 917504 | tf_op jit(solution)/shard_map/all_to_all | solution.py:132
  36.6 38.9 %all-gather.14.cloned.1.call-done = bf16[32,33,1024]{2,1,0:T(8,128)(2,1)} async-done(((bf16[1,33,1024]{2,1,0:T(8,128)(2,1)}), bf16[32,33,1024]{2,1,0:T(8,128)(2,1)}) %all-gather.14.cloned.1.call-update) | async-done | bytes 2162704 | tf_op jit(solution)/shard_map/all_gather | solution.py:143
  82.3 36.3 %all-gather.8.cloned.1.call-done = bf16[1280,2176]{1,0:T(8,128)(2,1)} async-done(((bf16[160,2176]{1,0:T(8,128)(2,1)}), bf16[1280,2176]{1,0:T(8,128)(2,1)}) %all-gather.8.cloned.1.call-update) | async-done | bytes 5570576 | tf_op jit(solution)/shard_map/all_gather | solution.py:115
  123.4 38.2 %all-gather.12.cloned.1.call-done = bf16[32,32,896]{2,1,0:T(8,128)(2,1)} async-done(((bf16[8,32,896]{2,1,0:T(8,128)(2,1)}), bf16[32,32,896]{2,1,0:T(8,128)(2,1)}) %all-gather.12.cloned.1.call-update) | async-done | bytes 1835024 | tf_op jit(solution)/shard_map/all_gather | solution.py:133
  161.6 3.5 fusion.160
  167.0 5.9 %fusion.69 = bf16[1280,256]{0,1:T(8,128)(2,1)S(1)} fusion(f32[1280,384]{0,1:T(8,128)S(1)} %get-tuple-element.69, f32[1280,8]{0,1:T(8,128)S(1)} %get-tuple-element.33, f32[1280,248]{0,1:T(8,128)S(1)} %get-tuple-element.35, f32[1280,248]{0,1:T(8,128)S(1)} %get-tuple-element.34, f32[1280,8]{0,1:T(8,128)S(1)} %get-tuple-element.32, ...), kind=kLoop, calls=%fused_computation.83 | loop fusion | flops 3932160 | bytes 4594176 | tf_op jit(solution)/shard_map/convert_element_type | solution.py:162
  182.9 5.0 %multiply_convert_fusion.1 = (bf16[1280,512]{1,0:T(8,128)(2,1)}, f32[1280,512]{1,0:T(8,128)}) fusion(f32[512]{0:T(512)S(1)} %bitcast.213, bf16[1024,896]{1,0:T(8,128)(2,1)S(1)} %bitcast.218, f32[1024]{0:T(1024)S(1)} %copy-done.32, f32[1024]{0:T(1024)S(1)} %copy-done.30, f32[1280]{0:T(1024)S(1)} %copy-done.24, f32[1280]{0:T(1024)S(1)} %broadcast_multiply_fusion, ...), kind=kOutput, calls=%fused_computation.45 | convolution fusion | flops 1353973760 | bytes 7628800 | tf_op jit(solution)/shard_map/dot_general | solution.py:168
  187.9 4.6 all-gather.10.cloned.1.call-done
  192.5 5.4 %fusion.161 = (f32[512]{0:T(512)S(1)}, bf16[1280,512]{1,0:T(8,128)(2,1)S(1)}) fusion(f32[1280,512]{1,0:T(8,128)} %get-tuple-element.73, bf16[512,1024]{1,0:T(8,128)(2,1)} %all-gather.10.cloned.1.call-done, bf16[1280,2176]{1,0:T(8,128)(2,1)} %all-gather.8.cloned.1.call-done), kind=kOutput, calls=%fused_computation.257 | convolution fusion | flops 1349385728 | bytes 7604224 | tf_op jit(solution)/shard_map/dot_general | solution.py:77
  198.0 3.9 fusion.94
  216.2 4.9 convolution_convert_fusion.1
  221.1 4.4 fusion.88
  225.5 6.5 %convolution_bitcast_fusion = f32[5,768,2,64]{1,3,2,0:T(8,128)} fusion(bf16[5,256,2,64]{1,3,2,0:T(8,128)(2,1)S(1)} %constant_dynamic-update-slice_fusion.15, f32[5,2,256,768]{3,2,1,0:T(8,128)} %copy-done, f32[5,2,256]{2,1,0:T(2,128)S(1)} %log_add_fusion, pred[5,256,768]{2,1,0:T(8,128)(4,1)S(1)} %compare_and_fusion), kind=kOutput, calls=%fused_computation.75 | convolution fusion | flops 259522560 | bytes 11151360 | tf_op jit(solution)/shard_map/nhqk,nhqd->nhkd/dot_general | solution.py:228
  232.0 4.2 reshape.393
  236.2 5.4 %fusion.151 = (f32[5,1,256,128]{2,1,3,0:T(1,128)S(1)}, f32[5,1,256,128]{2,1,3,0:T(1,128)S(1)}, f32[5,1,256,128]{2,1,3,0:T(1,128)S(1)}) fusion(f32[5,3,256,128]{2,1,3,0:T(4,128)} %reshape.393), kind=kLoop, calls=%fused_computation.247 | loop fusion | bytes 3932160 | tf_op jit(solution)/shard_map/slice | solution.py:59
  242.5 21.8 %fusion.60 = f32[5,768,2,64]{1,3,2,0:T(8,128)} fusion(f32[5,2,256,768]{3,2,1,0:T(8,128)} %fusion.88, f32[5,2,256,768]{3,2,1,0:T(8,128)} %copy-done, f32[5,2,256]{2,1,0:T(2,128)S(1)} %log_add_fusion, pred[5,256,768]{2,1,0:T(8,128)(4,1)S(1)} %compare_and_fusion, bf16[5,256,2,64]{1,3,2,0:T(8,128)(2,1)} %copy-done.8), kind=kOutput, calls=%fused_computation.74 | convolution fusion | flops 273288448 | bytes 19015680 | tf_op jit(solution)/shard_map/nhqk,nhqd->nhkd/dot_general | solution.py:227
  264.4 4.2 reshape.391
  268.6 5.4 %fusion.152 = (f32[5,1,256,128]{2,1,3,0:T(1,128)S(1)}, f32[5,1,256,128]{2,1,3,0:T(1,128)S(1)}, f32[5,1,256,128]{2,1,3,0:T(1,128)S(1)}) fusion(f32[5,3,256,128]{2,1,3,0:T(4,128)} %reshape.391), kind=kLoop, calls=%fused_computation.248 | loop fusion | bytes 3932160 | tf_op jit(solution)/shard_map/slice | solution.py:59
  279.0 21.3 %fusion.80 = f32[5,256,2,64]{1,3,2,0:T(8,128)} fusion(f32[5,2,256,768]{3,2,1,0:T(8,128)} %fusion.88, f32[5,2,256,768]{3,2,1,0:T(8,128)} %copy-done, f32[5,2,256]{2,1,0:T(2,128)S(1)} %log_add_fusion, pred[5,256,768]{2,1,0:T(8,128)(4,1)S(1)} %compare_and_fusion, bf16[5,768,2,64]{1,3,2,0:T(8,128)(2,1)} %copy-done.3), kind=kOutput, calls=%fused_computation.94 | convolution fusion | flops 273288448 | bytes 18360320 | tf_op jit(solution)/shard_map/nhqk,nhkd->nhqd/dot_general | solution.py:226
  303.8 5.8 %fusion.72 = f32[1280,256]{0,1:T(8,128)S(1)} fusion(f32[1280,128]{0,1:T(8,128)S(1)} %get-tuple-element.38, f32[1280,128]{0,1:T(8,128)S(1)} %bitcast.155, f32[1280,8]{0,1:T(8,128)S(1)} %slice.400, f32[1280,248]{0,1:T(8,128)S(1)} %get-tuple-element.37, f32[1280,248]{0,1:T(8,128)S(1)} %get-tuple-element.36, f32[1280,8]{0,1:T(8,128)S(1)} %slice.401, ...), kind=kLoop, calls=%fused_computation.86 | loop fusion | flops 4259840 | bytes 5249536 | tf_op jit(solution)/shard_map/add | solution.py:44
  310.0 6.6 %fusion.14 = (bf16[1024]{0:T(1024)(128)(2,1)S(1)}, bf16[1024]{0:T(1024)(128)(2,1)S(1)}, bf16[1024]{0:T(1024)(128)(2,1)S(1)}, bf16[1024]{0:T(1024)(128)(2,1)S(1)}, bf16[1280,1024]{1,0:T(8,128)(2,1)}) fusion(f32[1280,1024]{1,0:T(8,128)} %fusion.94, f32[1280]{0:T(1024)S(1)} %copy-done.25, f32[1280]{0:T(1024)S(1)} %broadcast_multiply_fusion, ...), kind=kOutput, calls=%fused_computation.21 | convolution fusion | flops 1025634304 | bytes 13264896 | tf_op jit(solution)/shard_map/dot_general | solution.py:77
  322.2 4.3 fusion.63
  329.7 3.3 add_convert_fusion.1
  335.4 8.4 %all-to-all-start.2 = ((bf16[32,32,256]{2,1,0:T(8,128)(2,1)}), bf16[32,32,256]{2,1,0:T(8,128)(2,1)S(1)}, u32[]{:S(2)}, u32[]{:S(2)}) async-start(bf16[32,32,256]{2,1,0:T(8,128)(2,1)} %bitcast.49), calls=%async_computation.6 | async-start | bytes 1048576 | tf_op jit(solution)/shard_map/all_to_all | solution.py:216
  343.9 18.8 %all-to-all-done.2 = bf16[32,32,256]{2,1,0:T(8,128)(2,1)S(1)} async-done(((bf16[32,32,256]{2,1,0:T(8,128)(2,1)}), bf16[32,32,256]{2,1,0:T(8,128)(2,1)S(1)}, u32[]{:S(2)}, u32[]{:S(2)}) %all-to-all-start.2) | async-done | bytes 524320 | tf_op jit(solution)/shard_map/all_to_all | solution.py:216
  362.7 3.5 all-to-all-start.3
  368.3 4.8 all-to-all-done.3
  373.2 3.4 all-to-all-start.1
  378.2 7.9 %reduce-scatter.17.cloned.1.call-done = bf16[128,1024]{1,0:T(8,128)(2,1)} async-done(((bf16[512,1024]{1,0:T(8,128)(2,1)}), bf16[128,1024]{1,0:T(8,128)(2,1)}) %reduce-scatter.17.cloned.1.call-update) | async-done | bytes 262160 | tf_op jit(solution)/shard_map/reduce_scatter | solution.py:178
  393.1 38.5 %reduce-scatter.9.cloned.1.call-done = bf16[160,1024]{1,0:T(8,128)(2,1)} async-done(((bf16[1280,1024]{1,0:T(8,128)(2,1)}), bf16[160,1024]{1,0:T(8,128)(2,1)}) %reduce-scatter.9.cloned.1.call-update) | async-done | bytes 327696 | tf_op jit(solution)/shard_map/reduce_scatter | solution.py:244
  432.9 45.4 %reduce-scatter.7.cloned.1.call-done = bf16[160,1024]{1,0:T(8,128)(2,1)} async-done(((bf16[1280,1024]{1,0:T(8,128)(2,1)}), bf16[160,1024]{1,0:T(8,128)(2,1)}) %reduce-scatter.7.cloned.1.call-update) | async-done | bytes 327696 | tf_op jit(solution)/shard_map/reduce_scatter | solution.py:207
  (284 shorter events, 81.8 us)
Async XLA Ops:
  7.2 11.3 %copy-start.19 = (bf16[32,3072]{1,0:T(8,128)(2,1)S(1)}, bf16[32,3072]{1,0:T(8,128)(2,1)}, u32[]{:S(2)}) copy-start(bf16[32,3072]{1,0:T(8,128)(2,1)} %param.18) | copy-start | bytes 589828
  7.2 68.3 %all-gather.14.cloned.1.call-start = ((), (), s32[]{:S(2)}) async-start(), calls=%async_computation.19 | async-start | bytes 2703360 | tf_op jit(solution)/shard_map/all_gather | solution.py:143
  14.2 104.4 %all-gather.8.cloned.1.call-start = ((), (), s32[]{:S(2)}) async-start(), calls=%async_computation.10 | async-start | bytes 6266880 | tf_op jit(solution)/shard_map/all_gather | solution.py:115
  17.2 144.4 %all-gather.12.cloned.1.call-start = ((), (), s32[]{:S(2)}) async-start(), calls=%async_computation.18 | async-start | bytes 2293760 | tf_op jit(solution)/shard_map/all_gather | solution.py:133
  18.3 16.9 %copy-start.2 = (bf16[160,1024]{1,0:T(8,128)(2,1)S(1)}, bf16[160,1024]{1,0:T(8,128)(2,1)}, u32[]{:S(2)}) copy-start(bf16[160,1024]{1,0:T(8,128)(2,1)} %param.29) | copy-start | bytes 983044
  33.6 158.9 %all-gather.10.cloned.1.call-start = ((), (), s32[]{:S(2)}) async-start(), calls=%async_computation.11 | async-start | bytes 1310720 | tf_op jit(solution)/shard_map/all_gather | solution.py:136
  34.1 298.9 %reduce-scatter.13.cloned.1.call-start = ((), (), s32[]{:S(2)}) async-start(), calls=%async_computation.15 | async-start | bytes 327680 | tf_op jit(solution)/shard_map/reduce_scatter | solution.py:211
  34.2 132.7 %copy-start.36 = (pred[256]{0:T(512)(128)(4,1)}, pred[256]{0:T(512)(128)(4,1)S(1)}, u32[]{:S(2)}) copy-start(pred[256]{0:T(512)(128)(4,1)S(1)} %get-tuple-element.76) | copy-start | bytes 772
  34.2 132.7 %copy-start.38 = (pred[256]{0:T(512)(128)(4,1)}, pred[256]{0:T(512)(128)(4,1)S(1)}, u32[]{:S(2)}) copy-start(pred[256]{0:T(512)(128)(4,1)S(1)} %get-tuple-element.77) | copy-start | bytes 772
  34.2 132.7 %copy-start.34 = (f32[256]{0:T(256)}, f32[256]{0:T(256)S(1)}, u32[]{:S(2)}) copy-start(f32[256]{0:T(256)S(1)} %compare_select_fusion.2) | copy-start | bytes 3076
  35.3 85.4 %copy-start.40 = (f32[8]{0:T(128)}, f32[8]{0:T(128)S(1)}, u32[]{:S(2)}) copy-start(f32[8]{0:T(128)S(1)} %compare_convert_fusion) | copy-start | bytes 100
  76.7 44.1 %copy-start.10 = (bf16[32,1,1024]{2,0,1:T(8,128)(2,1)}, bf16[32,1,1024]{2,0,1:T(8,128)(2,1)S(1)}, u32[]{:S(2)}) copy-start(bf16[32,1,1024]{2,0,1:T(8,128)(2,1)S(1)} %copy.167) | copy-start | bytes 196612
  77.1 84.5 %copy-start.26 = (f32[1024]{0:T(1024)}, f32[1024]{0:T(1024)S(1)}, u32[]{:S(2)}) copy-start(f32[1024]{0:T(1024)S(1)} %reshape.408) | copy-start | bytes 12292
  77.1 84.4 %copy-start.28 = (f32[1024]{0:T(1024)}, f32[1024]{0:T(1024)S(1)}, u32[]{:S(2)}) copy-start(f32[1024]{0:T(1024)S(1)} %reshape.409) | copy-start | bytes 12292
  123.4 41.7 %copy-start.23 = (f32[1280]{0:T(1024)}, f32[1280]{0:T(1024)S(1)}, u32[]{:S(2)}) copy-start(f32[1280]{0:T(1024)S(1)} %add_rsqrt_fusion) | copy-start | bytes 15364
  165.1 8.9 %copy-start.4 = (bf16[1280,384]{0,1:T(8,128)(2,1)}, bf16[1280,384]{0,1:T(8,128)(2,1)S(1)}, u32[]{:S(2)}) copy-start(bf16[1280,384]{0,1:T(8,128)(2,1)S(1)} %get-tuple-element.68) | copy-start | bytes 2949124
  174.8 29.4 %collective-permute-start = (bf16[512,256]{0,1:T(8,128)(2,1)}, bf16[512,256]{0,1:T(8,128)(2,1)}, u32[]{:S(2)}, u32[]{:S(2)}) collective-permute-start(bf16[512,256]{0,1:T(8,128)(2,1)} %pad_maximum_fusion.4), channel_id=1, source_target_pairs={{0,8},{8,16},{16,24},{1,9},{9,17},{17,25},{2,10},{10,18},{18,26},{... | collective-permute-start | bytes 786440 | tf_op jit(solution)/shard_map/ppermute | solution.py:166
  216.1 146.6 %reduce-scatter.15.cloned.1.call-start = ((), (), s32[]{:S(2)}) async-start(), calls=%async_computation.16 | async-start | bytes 1310720 | tf_op jit(solution)/shard_map/reduce_scatter | solution.py:179
  221.1 145.5 %reduce-scatter.11.cloned.1.call-start = ((), (), s32[]{:S(2)}) async-start(), calls=%async_computation.14 | async-start | bytes 1310720 | tf_op jit(solution)/shard_map/reduce_scatter | solution.py:263
  277.7 24.3 %collective-permute-start.1 = (bf16[512,256]{0,1:T(8,128)(2,1)}, bf16[512,256]{0,1:T(8,128)(2,1)}, u32[]{:S(2)}, u32[]{:S(2)}) collective-permute-start(bf16[512,256]{0,1:T(8,128)(2,1)} %fusion.114), channel_id=1, source_target_pairs={{8,0},{16,8},{24,16},{9,1},{17,9},{25,17},{10,2},{18,10},{26,18},{... | collective-permute-start | bytes 786440 | tf_op jit(solution)/shard_map/ppermute | solution.py:234
  303.8 6.2 %copy-start.27 = (f32[1024]{0:T(1024)S(1)}, f32[1024]{0:T(1024)}, u32[]{:S(2)}) copy-start(f32[1024]{0:T(1024)} %copy-done.26) | copy-start | bytes 12292
  310.0 6.9 %copy-start.21 = (bf16[32,32]{1,0:T(8,128)(2,1)S(1)}, bf16[32,32]{1,0:T(8,128)(2,1)}, u32[]{:S(2)}) copy-start(bf16[32,32]{1,0:T(8,128)(2,1)} %reshape.399) | copy-start | bytes 6148
  310.0 6.9 %copy-start.22 = (bf16[32,128]{1,0:T(8,128)(2,1)S(1)}, bf16[32,128]{1,0:T(8,128)(2,1)}, u32[]{:S(2)}) copy-start(bf16[32,128]{1,0:T(8,128)(2,1)} %fusion.124) | copy-start | bytes 24580
  310.0 7.3 %copy-start.29 = (f32[1024]{0:T(1024)S(1)}, f32[1024]{0:T(1024)}, u32[]{:S(2)}) copy-start(f32[1024]{0:T(1024)} %copy-done.28) | copy-start | bytes 12292
  321.7 64.5 %reduce-scatter.17.cloned.1.call-start = ((), (), s32[]{:S(2)}) async-start(), calls=%async_computation.17 | async-start | bytes 1310720 | tf_op jit(solution)/shard_map/reduce_scatter | solution.py:178
  326.5 105.1 %reduce-scatter.9.cloned.1.call-start = ((), (), s32[]{:S(2)}) async-start(), calls=%async_computation.13 | async-start | bytes 2949120 | tf_op jit(solution)/shard_map/reduce_scatter | solution.py:244
  327.2 151.1 %reduce-scatter.7.cloned.1.call-start = ((), (), s32[]{:S(2)}) async-start(), calls=%async_computation.12 | async-start | bytes 2949120 | tf_op jit(solution)/shard_map/reduce_scatter | solution.py:207
  333.0 10.8 %copy-start.1 = (bf16[160,1024]{1,0:T(8,128)(2,1)S(1)}, bf16[160,1024]{1,0:T(8,128)(2,1)}, u32[]{:S(2)}) copy-start(bf16[160,1024]{1,0:T(8,128)(2,1)} %param.15) | copy-start | bytes 983044
  335.4 27.3 %all-to-all-start.2 = ((bf16[32,32,256]{2,1,0:T(8,128)(2,1)}), bf16[32,32,256]{2,1,0:T(8,128)(2,1)S(1)}, u32[]{:S(2)}, u32[]{:S(2)}) async-start(bf16[32,32,256]{2,1,0:T(8,128)(2,1)} %bitcast.49), calls=%async_computation.6 | async-start | bytes 1048576 | tf_op jit(solution)/shard_map/all_to_all | solution.py:216
  362.7 10.5 %all-to-all-start.3 = ((bf16[8,32,512]{2,1,0:T(8,128)(2,1)}), bf16[8,32,512]{2,1,0:T(8,128)(2,1)S(1)}, u32[]{:S(2)}, u32[]{:S(2)}) async-start(bf16[8,32,512]{2,1,0:T(8,128)(2,1)} %bitcast.209), calls=%async_computation.8 | async-start | bytes 524288 | tf_op jit(solution)/shard_map/all_to_all | solution.py:180
  373.2 16.4 %all-to-all-start.1 = ((bf16[8,32,512]{2,1,0:T(8,128)(2,1)}), bf16[8,32,512]{2,1,0:T(8,128)(2,1)S(1)}, u32[]{:S(2)}, u32[]{:S(2)}) async-start(bf16[8,32,512]{2,1,0:T(8,128)(2,1)} %bitcast.46), calls=%async_computation.4 | async-start | bytes 524288 | tf_op jit(solution)/shard_map/all_to_all | solution.py:264
  393.1 88.0 %copy-start.44 = (f32[32]{0:T(128)}, f32[32]{0:T(128)S(1)}, u32[]{:S(2)}) copy-start(f32[32]{0:T(128)S(1)} %get-tuple-element.107) | copy-start | bytes 388
  (34 other events, 110.7 us)
Sparse Core Ops, SparseCore 0:
  14.4 61.1 all-gather.13
  77.4 41.1 all-gather.7
  120.2 41.3 all-gather.11
  163.0 29.4 all-gather.9
  216.2 21.9 reduce-scatter.12
  240.4 25.5 reduce-scatter.14
  321.8 34.2 reduce-scatter.10
  358.4 27.7 reduce-scatter.16
  389.5 42.0 reduce-scatter.8
  434.8 43.4 reduce-scatter.6
